TPU v7x, 32 devices: a whole 2x2x4 slice. The times are simulated.
32 devices in a mesh: ctx: 4 (over x, core), fsdp: 8 (over z, y).
Axes of the slice: x: 2, y: 2, z: 4, core: 2. Of those that a mesh axis runs over, the one named last changes fastest.
Arguments:
- inputs: bfloat16 [2, 8, 512, 1024], P(None, 'fsdp', 'ctx'), may hold values from -6 to 6
- cotangent: bfloat16 [2, 8, 512, 1024], P(None, 'fsdp', 'ctx'), may hold values from -6 to 6
- lengths: int32 [2, 8], P(None, 'fsdp'), may hold values from 128 to 512, as said below
- query_weight: bfloat16 [1024, 1024], P('fsdp'), may hold values from -0.1875 to 0.1875
- key_weight: bfloat16 [1024, 1024], P('fsdp'), may hold values from -0.1875 to 0.1875
- value_weight: bfloat16 [1024, 1024], P('fsdp'), may hold values from -0.1875 to 0.1875
- output_weight: bfloat16 [1024, 1024], P('fsdp'), may hold values from -0.75 to 0.75
- query_bias: bfloat16 [1024], P('fsdp'), may hold values from -3 to 3
- value_bias: bfloat16 [1024], P('fsdp'), may hold values from -3 to 3
- output_bias: bfloat16 [1024], P('fsdp'), may hold values from -2 to 2
- first_gain: bfloat16 [1024], P('fsdp'), may hold values from 0.099609375 to 1.8984375
- first_shift: bfloat16 [1024], P('fsdp'), may hold values from -2 to 2
- inner_weight: bfloat16 [1024, 4096], P('fsdp'), may hold values from -0.1875 to 0.1875
- inner_bias: bfloat16 [4096], P('fsdp'), may hold values from -3 to 3
- outer_weight: bfloat16 [4096, 1024], P('fsdp'), may hold values from -0.09375 to 0.09375
- outer_bias: bfloat16 [1024], P('fsdp'), may hold values from -2 to 2
- second_gain: bfloat16 [1024], P('fsdp'), may hold values from 0.099609375 to 1.8984375
- second_shift: bfloat16 [1024], P('fsdp'), may hold values from -2 to 2
Outputs:
- layer_output: bfloat16 [2, 8, 512, 1024], P(None, 'fsdp', 'ctx')
- input_gradient: float32 [2, 8, 512, 1024], P(None, 'fsdp', 'ctx')
- query_weight_gradient: float32 [1024, 1024], P('fsdp')
- key_weight_gradient: float32 [1024, 1024], P('fsdp')
- value_weight_gradient: float32 [1024, 1024], P('fsdp')
- output_weight_gradient: float32 [1024, 1024], P('fsdp')
- query_bias_gradient: float32 [1024], P('fsdp')
- value_bias_gradient: float32 [1024], P('fsdp')
- output_bias_gradient: float32 [1024], P('fsdp')
- first_gain_gradient: float32 [1024], P('fsdp')
- first_shift_gradient: float32 [1024], P('fsdp')
- inner_weight_gradient: float32 [1024, 4096], P('fsdp')
- inner_bias_gradient: float32 [4096], P('fsdp')
- outer_weight_gradient: float32 [4096, 1024], P('fsdp')
- outer_bias_gradient: float32 [1024], P('fsdp')
- second_gain_gradient: float32 [1024], P('fsdp')
- second_shift_gradient: float32 [1024], P('fsdp')
Inputs may be any that keep to these rules, and one draw needn't show every extreme that they name: The valid slots of a sequence are its first lengths entries; in every micro-batch some sequence fills all 512 slots.
All inputs are finite; a program needn't handle non-finite values.
Results may differ from a plain program's by a relative error of at most 0.018.
Values may be sent and summed in bfloat16 or wider, within the bound.
A program may use at most 256 MiB of HBM per device.

v0:
```python
import jax
import jax.numpy as jnp
from jax import lax
from jax.sharding import PartitionSpec as P

HEAD_DIM = 64
EPSILON = 1e-06
F32 = jnp.float32
BF16 = jnp.bfloat16


def exact_gelu(hidden):
    return jax.nn.gelu(hidden, approximate=False)


def plain_product(left, right):
    return jnp.dot(left, right, preferred_element_type=F32)


def left_product(left, right):
    return lax.dot_general(left, right, (((0,), (0,)), ((), ())), preferred_element_type=F32)


def right_product(left, right):
    return lax.dot_general(left, right, (((1,), (1,)), ((), ())), preferred_element_type=F32)


def column_sums(rows):
    return jnp.sum(rows.astype(F32), axis=0)


def norm_parts(total):
    average = jnp.mean(total, axis=-1, keepdims=True)
    centered = total - average
    variance = jnp.mean(centered * centered, axis=-1, keepdims=True)
    rate = lax.rsqrt(variance + EPSILON)
    return (centered * rate, rate)


def norm_back(unit, rate, grad):
    return rate * (
        grad
        - jnp.mean(grad, axis=-1, keepdims=True)
        - unit * jnp.mean(grad * unit, axis=-1, keepdims=True)
    )


def split_columns(packed, widths):
    pieces = []
    start = 0
    for width in widths:
        pieces.append(packed[..., start : start + width])
        start += width
    return pieces


def attention_forward(queries, keys_all, values_all, key_valid, heads):
    shape = queries.shape[:2] + (heads, HEAD_DIM)
    key_shape = keys_all.shape[:2] + (heads, HEAD_DIM)
    scores = jnp.einsum(
        "sqhd,skhd->shqk",
        queries.reshape(shape),
        keys_all.reshape(key_shape),
        preferred_element_type=F32,
    ) * HEAD_DIM ** (-0.5)
    scores = jnp.where(key_valid[:, None, None, :], scores, -1e30)
    top = jnp.max(scores, axis=-1, keepdims=True)
    weights = jnp.exp(scores - top)
    probs = (weights / jnp.sum(weights, axis=-1, keepdims=True)).astype(BF16)
    context = jnp.einsum(
        "shqk,skhd->sqhd", probs, values_all.reshape(key_shape), preferred_element_type=F32
    )
    return (context.reshape(queries.shape).astype(BF16), probs)


def attention_backward(queries, keys_all, values_all, probs, context_grad, heads):
    shape = queries.shape[:2] + (heads, HEAD_DIM)
    key_shape = keys_all.shape[:2] + (heads, HEAD_DIM)
    scale = HEAD_DIM ** (-0.5)
    grad_heads = context_grad.reshape(shape)
    wide = probs.astype(F32)
    probs_grad = jnp.einsum(
        "sqhd,skhd->shqk", grad_heads, values_all.reshape(key_shape), preferred_element_type=F32
    )
    inner_total = jnp.sum(wide * probs_grad, axis=-1, keepdims=True)
    scores_grad = (wide * (probs_grad - inner_total)).astype(BF16)
    query_grad = jnp.einsum(
        "shqk,skhd->sqhd", scores_grad, keys_all.reshape(key_shape), preferred_element_type=F32
    )
    key_part = jnp.einsum(
        "shqk,sqhd->skhd", scores_grad, queries.reshape(shape), preferred_element_type=F32
    )
    value_part = jnp.einsum("shqk,sqhd->skhd", probs, grad_heads, preferred_element_type=F32)
    return (
        (query_grad * scale).astype(BF16).reshape(queries.shape),
        (key_part * scale).astype(BF16).reshape(keys_all.shape),
        value_part.astype(BF16).reshape(values_all.shape),
    )


def gather_rows(part):
    return lax.all_gather(part, "fsdp", axis=0, tiled=True)


def reduce_rows(part):
    share = lax.psum_scatter(part.astype(BF16), "fsdp", scatter_dimension=0, tiled=True)
    return lax.psum(share, "ctx").astype(F32)


def body(
    inputs,
    cotangent,
    lengths,
    query_weight,
    key_weight,
    value_weight,
    output_weight,
    query_bias,
    value_bias,
    output_bias,
    first_gain,
    first_shift,
    inner_weight,
    inner_bias,
    outer_weight,
    outer_bias,
    second_gain,
    second_shift,
):
    vectors = (
        query_bias,
        value_bias,
        output_bias,
        first_gain,
        first_shift,
        inner_bias,
        outer_bias,
        second_gain,
        second_shift,
    )
    widths = [member.shape[0] for member in vectors]
    packed = lax.all_gather(jnp.concatenate(vectors), "fsdp", axis=0, tiled=False)
    (
        bias_query,
        bias_value,
        bias_output,
        gain_first,
        shift_first,
        bias_inner,
        bias_outer,
        gain_second,
        shift_second,
    ) = [piece.reshape(-1).astype(F32) for piece in split_columns(packed, widths)]
    full_qkv = gather_rows(jnp.concatenate((query_weight, key_weight, value_weight), axis=1))
    full_output = gather_rows(output_weight)
    full_inner = gather_rows(inner_weight)
    full_outer = gather_rows(outer_weight)
    micro, seqs, block_len, width = inputs.shape
    heads = width // HEAD_DIM
    ctx_size = lax.axis_size("ctx")
    total_slots = block_len * ctx_size
    group = micro * seqs
    rows = group * block_len
    flat_len = lengths.reshape(group)
    local_pos = lax.axis_index("ctx") * block_len + jnp.arange(block_len, dtype=jnp.int32)
    row_mask = (local_pos[None, :] < flat_len[:, None]).astype(F32).reshape(rows, 1)
    key_valid = jnp.arange(total_slots, dtype=jnp.int32)[None, :] < flat_len[:, None]
    flat_rows = inputs.reshape(rows, width)
    qkv = plain_product(flat_rows, full_qkv)
    queries = (qkv[:, :width] + bias_query).astype(BF16)
    keys_values = jnp.concatenate(
        (qkv[:, width : 2 * width], qkv[:, 2 * width :] + bias_value), axis=1
    ).astype(BF16)
    keys_values_all = lax.all_gather(
        keys_values.reshape(group, block_len, 2 * width), "ctx", axis=1, tiled=True
    )
    keys_all = keys_values_all[:, :, :width]
    values_all = keys_values_all[:, :, width:]
    queries3 = queries.reshape(group, block_len, width)
    context, probs = attention_forward(queries3, keys_all, values_all, key_valid, heads)
    context = context.reshape(rows, width)
    first_sum = flat_rows.astype(F32) + plain_product(context, full_output) + bias_output
    first_unit, first_rate = norm_parts(first_sum)
    normed = first_unit * gain_first + shift_first
    normed_low = normed.astype(BF16)
    hidden = plain_product(normed_low, full_inner) + bias_inner
    active, gelu_back = jax.vjp(exact_gelu, hidden)
    active_low = active.astype(BF16)
    second_sum = normed + plain_product(active_low, full_outer) + bias_outer
    second_unit, second_rate = norm_parts(second_sum)
    output = ((second_unit * gain_second + shift_second) * row_mask).astype(BF16)
    out_grad = cotangent.reshape(rows, width).astype(F32) * row_mask
    second_gain_part = jnp.sum(out_grad * second_unit, axis=0)
    second_shift_part = jnp.sum(out_grad, axis=0)
    second_grad = norm_back(second_unit, second_rate, out_grad * gain_second)
    second_low = second_grad.astype(BF16)
    outer_weight_part = left_product(active_low, second_low).astype(BF16)
    outer_bias_part = column_sums(second_low)
    (hidden_grad,) = gelu_back(right_product(second_low, full_outer))
    hidden_low = hidden_grad.astype(BF16)
    inner_weight_part = left_product(normed_low, hidden_low).astype(BF16)
    inner_bias_part = column_sums(hidden_low)
    normed_grad = second_grad + right_product(hidden_low, full_inner)
    first_gain_part = jnp.sum(normed_grad * first_unit, axis=0)
    first_shift_part = jnp.sum(normed_grad, axis=0)
    first_grad = norm_back(first_unit, first_rate, normed_grad * gain_first)
    branch_low = first_grad.astype(BF16)
    output_weight_part = left_product(context, branch_low).astype(BF16)
    output_bias_part = column_sums(branch_low)
    context_grad = right_product(branch_low, full_output).astype(BF16)
    query_grad, key_part, value_part = attention_backward(
        queries3, keys_all, values_all, probs, context_grad.reshape(queries3.shape), heads
    )
    keys_values_grad = lax.psum_scatter(
        jnp.concatenate((key_part, value_part), axis=2), "ctx", scatter_dimension=1, tiled=True
    ).reshape(rows, 2 * width)
    qkv_grad = jnp.concatenate((query_grad.reshape(rows, width), keys_values_grad), axis=1)
    qkv_weight_part = left_product(flat_rows, qkv_grad).astype(BF16)
    query_bias_part = column_sums(qkv_grad[:, :width])
    value_bias_part = column_sums(qkv_grad[:, 2 * width :])
    input_grad = first_grad + right_product(qkv_grad, full_qkv)
    qkv_share = reduce_rows(qkv_weight_part)
    output_share = reduce_rows(output_weight_part)
    inner_share = reduce_rows(inner_weight_part)
    outer_share = reduce_rows(outer_weight_part)
    vector_parts = (
        query_bias_part,
        value_bias_part,
        output_bias_part,
        first_gain_part,
        first_shift_part,
        inner_bias_part,
        outer_bias_part,
        second_gain_part,
        second_shift_part,
    )
    fsdp_size = lax.axis_size("fsdp")
    packed_parts = jnp.concatenate([part.reshape(fsdp_size, -1) for part in vector_parts], axis=1)
    vector_share = lax.psum(
        lax.psum_scatter(packed_parts, "fsdp", scatter_dimension=0, tiled=True), "ctx"
    )[0]
    shares = split_columns(vector_share, widths)
    query_share, key_share, value_share = split_columns(qkv_share, [width] * 3)
    return (
        output.reshape(inputs.shape),
        input_grad.reshape(inputs.shape),
        query_share,
        key_share,
        value_share,
        output_share,
        shares[0],
        shares[1],
        shares[2],
        shares[3],
        shares[4],
        inner_share,
        shares[5],
        outer_share,
        shares[6],
        shares[7],
        shares[8],
    )


def solution(mesh):
    data = P(None, "fsdp", "ctx", None)
    matrix = P("fsdp", None)
    vector = P("fsdp")
    return jax.shard_map(
        body,
        mesh=mesh,
        in_specs=(data, data, P(None, "fsdp"))
        + (matrix,) * 4
        + (vector,) * 5
        + (matrix, vector, matrix, vector, vector, vector),
        out_specs=(data, data)
        + (matrix,) * 4
        + (vector,) * 5
        + (matrix, vector, matrix, vector, vector, vector),
        check_vma=False,
    )
```

profile of v0, /device:TPU:0, one launch (start us, length us, event | category | flops | bytes accessed | tf_op | source)
XLA Modules:
  0.0 1151.7 jit_solution(14489153221293311323)
XLA Ops:
  7.2 2.0 pad_maximum_fusion.5
  16.9 33.0 %all-gather.1 = bf16[8,1,1536]{2,1,0:T(2,128)(2,1)S(1)} all-gather(bf16[1,1,1536]{2,1,0:T(2,128)(2,1)S(1)} %reshape.321), channel_id=2, replica_groups=mesh['ctx'=4,'fsdp'=8] {'fsdp'}, dimensions={0}, use_global_device_ids=true | all-gather | bytes 27648 | tf_op jit(solution)/shard_map/all_gather | solution.py:142
  50.0 63.2 %all-gather.8.cloned.1.call-done = bf16[1024,3072]{1,0:T(8,128)(2,1)} async-done(((bf16[128,3072]{1,0:T(8,128)(2,1)}), bf16[1024,3072]{1,0:T(8,128)(2,1)}) %all-gather.8.cloned.1.call-update) | async-done | bytes 6291472 | tf_op jit(solution)/shard_map/all_gather | solution.py:102
  113.1 4.8 convolution_bitcast_fusion
  122.5 1.6 copy.67
  124.1 28.1 %all-gather.10.cloned.1.call-done = bf16[2,512,2048]{2,1,0:T(8,128)(2,1)} async-done(((bf16[2,128,2048]{2,1,0:T(8,128)(2,1)}), bf16[2,512,2048]{2,1,0:T(8,128)(2,1)}) %all-gather.10.cloned.1.call-update) | async-done | bytes 4194320 | tf_op jit(solution)/shard_map/all_gather | solution.py:174
  152.1 4.2 fusion.52
  156.4 2.7 copy.66
  159.1 2.9 copy.64
  162.0 7.7 fusion.54
  169.7 3.9 divide_convert_fusion
  173.6 2.0 copy-done
  178.5 25.1 %all-gather.12.cloned.1.call-done = bf16[1024,1024]{1,0:T(8,128)(2,1)} async-done(((bf16[128,1024]{1,0:T(8,128)(2,1)}), bf16[1024,1024]{1,0:T(8,128)(2,1)}) %all-gather.12.cloned.1.call-update) | async-done | bytes 2097168 | tf_op jit(solution)/shard_map/all_gather | solution.py:102
  203.6 2.7 fusion.55
  206.5 122.5 %all-gather.14.cloned.1.call-done = bf16[1024,4096]{1,0:T(8,128)(2,1)} async-done(((bf16[128,4096]{1,0:T(8,128)(2,1)}), bf16[1024,4096]{1,0:T(8,128)(2,1)}) %all-gather.14.cloned.1.call-update) | async-done | bytes 8388624 | tf_op jit(solution)/shard_map/all_gather | solution.py:102
  329.0 16.2 %multiply_convert_fusion.1 = (bf16[256,4096]{1,0:T(8,128)(2,1)}, f32[256,4096]{1,0:T(8,128)}, f32[256,4096]{1,0:T(8,128)}) fusion(f32[4096]{0:T(1024)S(1)} %bitcast.181, bf16[1024,4096]{1,0:T(8,128)(2,1)} %all-gather.14.cloned.1.call-done, f32[256,1024]{1,0:T(8,128)S(1)} %get-tuple-element.115, f32[1024]{0:T(1024)S(1)} %get-tuple-element.97, ...), kind=kOutput, calls=%fused_computation.19 | convolution fusion | flops 2218000384 | bytes 19949568 | tf_op jit(solution)/shard_map/dot_general | solution.py:17
  345.3 108.9 %all-gather.16.cloned.1.call-done = bf16[4096,1024]{1,0:T(8,128)(2,1)} async-done(((bf16[512,1024]{1,0:T(8,128)(2,1)}), bf16[4096,1024]{1,0:T(8,128)(2,1)}) %all-gather.16.cloned.1.call-update) | async-done | bytes 8388624 | tf_op jit(solution)/shard_map/all_gather | solution.py:102
  454.2 6.5 fusion.56
  462.9 11.1 convert_reduce_fusion
  474.1 6.9 multiply_reduce_fusion.1
  482.3 1.6 convolution_convert_fusion.5
  483.9 2.9 reshape.329
  486.7 2.8 copy.70
  489.5 4.0 fusion.1
  494.2 4.3 fusion.2
  498.5 1.9 copy-done.2
  500.4 2.0 multiply_convert_fusion
  502.5 3.9 copy.74
  506.4 2.4 copy.75
  508.8 4.7 pad_maximum_fusion
  515.1 4.6 convert_reduce_fusion.4
  519.8 1.9 copy.82
  522.4 34.0 %reduce-scatter.8.cloned.1.call-done = bf16[2,128,2048]{2,1,0:T(8,128)(2,1)} async-done(((bf16[2,512,2048]{2,1,0:T(8,128)(2,1)}), bf16[2,128,2048]{2,1,0:T(8,128)(2,1)}) %reduce-scatter.8.cloned.1.call-update) | async-done | bytes 1048592 | tf_op jit(solution)/shard_map/reduce_scatter | solution.py:214
  556.4 5.9 convert_bitcast_fusion
  562.3 8.7 copy.83
  572.3 2.0 convolution_convert_fusion.3
  574.6 7.3 convolution_convert_fusion.1
  583.1 7.2 convolution_convert_fusion
  591.8 97.3 %reduce-scatter.16.cloned.1.call-done = bf16[128,3072]{1,0:T(8,128)(2,1)} async-done(((bf16[1024,3072]{1,0:T(8,128)(2,1)}), bf16[128,3072]{1,0:T(8,128)(2,1)}) %reduce-scatter.16.cloned.1.call-update) | async-done | bytes 786448
  689.1 2.3 copy.84
  691.4 69.1 %reduce-scatter.10.cloned.1.call-done = bf16[128,1024]{1,0:T(8,128)(2,1)} async-done(((bf16[1024,1024]{1,0:T(8,128)(2,1)}), bf16[128,1024]{1,0:T(8,128)(2,1)}) %reduce-scatter.10.cloned.1.call-update) | async-done | bytes 262160 | tf_op jit(solution)/shard_map/reduce_scatter | solution.py:106
  760.5 152.1 %reduce-scatter.12.cloned.1.call-done = bf16[128,4096]{1,0:T(8,128)(2,1)} async-done(((bf16[1024,4096]{1,0:T(8,128)(2,1)}), bf16[128,4096]{1,0:T(8,128)(2,1)}) %reduce-scatter.12.cloned.1.call-update) | async-done | bytes 1048592 | tf_op jit(solution)/shard_map/reduce_scatter | solution.py:106
  912.6 151.5 %reduce-scatter.14.cloned.1.call-done = bf16[512,1024]{1,0:T(8,128)(2,1)} async-done(((bf16[4096,1024]{1,0:T(8,128)(2,1)}), bf16[512,1024]{1,0:T(8,128)(2,1)}) %reduce-scatter.14.cloned.1.call-update) | async-done | bytes 1048592 | tf_op jit(solution)/shard_map/reduce_scatter | solution.py:106
  1064.2 35.6 %all-reduce = f32[8,1536]{1,0:T(8,128)S(1)} all-reduce(f32[8,1536]{1,0:T(8,128)S(1)} %constant_dynamic-update-slice_fusion), channel_id=6, replica_groups=mesh['ctx'=4,'fsdp'=8] {'fsdp'}, use_global_device_ids=true, to_apply=%region_25.26.clone | all-reduce | flops 12288 | bytes 98304
  1100.5 5.8 psum.37
  1107.3 5.9 convolution_add_fusion.2
  1113.3 22.2 %all-reduce.4.cloned.1.call-done = (bf16[128,3072]{0,1:T(8,128)(2,1)}, bf16[128,1024]{1,0:T(8,128)(2,1)}, bf16[128,4096]{1,0:T(8,128)(2,1)}, bf16[512,1024]{1,0:T(8,128)(2,1)}) async-done(((bf16[128,3072]{0,1:T(8,128)(2,1)}, bf16[128,1024]{1,0:T(8,128)(2,1)}, bf16[128,4096]{1,0:T(8,128)(2,1)}, bf16[512,1024]{1,0:T(8,128)(2,1)}), (bf16[128,3072]{0,1:T(8,128)(2,1)}, bf16[128,1024]{1,0:T(8,128)(2,1)}, ...) | async-done | bytes 3145744 | tf_op jit(solution)/shard_map/psum | solution.py:107
  1139.8 2.8 convert_element_type.278
  (125 shorter events, 34.4 us)
Async XLA Ops:
  7.2 105.9 %all-gather.8.cloned.1.call-start = ((), (), s32[]{:S(2)}) async-start(), calls=%async_computation.5 | async-start | bytes 7077888 | tf_op jit(solution)/shard_map/all_gather | solution.py:102
  9.3 142.8 %all-gather.10.cloned.1.call-start = ((), (), s32[]{:S(2)}) async-start(), calls=%async_computation.6 | async-start | bytes 5242880 | tf_op jit(solution)/shard_map/all_gather | solution.py:174
  118.0 3.4 copy-start.19
  118.0 3.4 copy-start.8
  119.3 84.3 %all-gather.12.cloned.1.call-start = ((), (), s32[]{:S(2)}) async-start(), calls=%async_computation.7 | async-start | bytes 2359296 | tf_op jit(solution)/shard_map/all_gather | solution.py:102
  120.1 209.0 %all-gather.14.cloned.1.call-start = ((), (), s32[]{:S(2)}) async-start(), calls=%async_computation.8 | async-start | bytes 9437184 | tf_op jit(solution)/shard_map/all_gather | solution.py:102
  120.6 333.5 %all-gather.16.cloned.1.call-start = ((), (), s32[]{:S(2)}) async-start(), calls=%async_computation.9 | async-start | bytes 9437184 | tf_op jit(solution)/shard_map/all_gather | solution.py:102
  121.2 435.2 %reduce-scatter.8.cloned.1.call-start = ((), (), s32[]{:S(2)}) async-start(), calls=%async_computation.10 | async-start | bytes 5242880 | tf_op jit(solution)/shard_map/reduce_scatter | solution.py:214
  159.1 2.9 copy-start.14
  173.6 2.0 copy-start
  454.2 6.8 copy-start.9
  460.7 2.2 copy-start.21
  462.8 11.2 copy-start.11
  474.0 6.9 copy-start.13
  474.0 8.3 copy-start.5
  481.3 1.0 copy-start.3
  489.5 4.0 copy-start.1
  489.5 4.0 copy-start.10
  494.2 6.2 copy-start.15
  498.5 1.9 copy-start.2
  513.5 1.6 copy-start.6
  513.6 175.6 %reduce-scatter.16.cloned.1.call-start = ((), (), s32[]{:S(2)}) async-start(), calls=%async_computation.14 | async-start | bytes 7077888
  570.9 1.2 copy-start.4
  570.9 1.4 copy-start.7
  571.0 189.6 %reduce-scatter.10.cloned.1.call-start = ((), (), s32[]{:S(2)}) async-start(), calls=%async_computation.11 | async-start | bytes 2359296 | tf_op jit(solution)/shard_map/reduce_scatter | solution.py:106
  574.3 338.3 %reduce-scatter.12.cloned.1.call-start = ((), (), s32[]{:S(2)}) async-start(), calls=%async_computation.12 | async-start | bytes 9437184 | tf_op jit(solution)/shard_map/reduce_scatter | solution.py:106
  581.9 1.2 copy-start.12
  581.9 482.2 %reduce-scatter.14.cloned.1.call-start = ((), (), s32[]{:S(2)}) async-start(), calls=%async_computation.13 | async-start | bytes 9437184 | tf_op jit(solution)/shard_map/reduce_scatter | solution.py:106
  590.3 0.7 copy-start.20
  590.3 1.3 copy-start.18
  590.3 545.2 %all-reduce.4.cloned.1.call-start = ((), (), s32[]{:S(2)}) async-start(), calls=%async_computation.15 | async-start | bytes 6291456 | tf_op jit(solution)/shard_map/psum | solution.py:107
  1135.5 7.1 copy-start.16
  1137.8 6.3 copy-start.17
Sparse Core Ops, SparseCore 0:
  10.8 102.3 all-gather.7
  119.5 32.6 all-gather.9
  154.3 49.2 all-gather.11
  205.6 123.4 all-gather.13
  331.0 123.1 all-gather.15
  513.7 42.6 reduce-scatter.7
  571.1 117.9 reduce-scatter.15
  693.6 66.8 reduce-scatter.9
  764.6 147.9 reduce-scatter.11
  916.1 147.9 reduce-scatter.13
  1067.4 68.0 all-reduce.3
where the time goes:
time: 1160 us; the launch traced here: 1150 us
  waiting for transfers between devices  876 us (76%)
  matrix products  98.7 us (9%)
  blocking collectives  74.4 us (6%)
  local copies, waits for them, and re-layouts  62.8 us (5%)
  other arithmetic  24.6 us (2%)
  between operations  14.5 us (1%)
    reduce_scatter x3, waiting for transfers between devices, reduce_rows(): lax.psum_scatter(part.astype(BF16), 'fsdp', scatter_dimension=0, tiled=True)  373 us
    all_gather x4, waiting for transfers between devices, gather_rows(): return lax.all_gather(part, 'fsdp', axis=0, tiled=True)  320 us
    unnamed x12, waiting for transfers between devices  99.2 us
    unnamed x1, blocking collectives  35.6 us
    reduce_scatter x1, waiting for transfers between devices, body(): lax.psum_scatter(jnp.concatenate((key_part, value_part), axis=2), 'ctx',...  34 us
    all_gather x1, blocking collectives, body(): lax.all_gather(jnp.concatenate(vectors), 'fsdp', axis=0, tiled=False)  33 us
    unnamed x70, local copies, waits for them, and re-layouts  31.4 us
    dot_general x4, matrix products, plain_product(): return jnp.dot(left, right, preferred_element_type=F32)  30.2 us
  transfers between devices with their start and end apart: 11, of which 11 were waited for; matrix products, arithmetic and copies ran while one was open for 8% of the time, Pallas kernels for 0%

commit v1 on v0

--- a/solution.py
+++ b/solution.py
@@ -1,3 +1,4 @@
+import functools
 import jax
 import jax.numpy as jnp
 from jax import lax
@@ -7,6 +8,39 @@
 EPSILON = 1e-06
 F32 = jnp.float32
 BF16 = jnp.bfloat16
+
+
+def solve_the_notes(patch, where_dim):
+    reached = list(patch.shape[1:])
+    reached[where_dim] *= patch.shape[0]
+    parts_out = jnp.moveaxis(patch, 0, where_dim).reshape(reached)
+    return parts_out
+
+
+def replace_panels(sheet, across):
+    spare, latest = (lax.axis_size(across), lax.axis_index(across))
+    a_next, small = (sheet[None], 1)
+    while small < spare:
+        in_order = []
+        k0 = 0
+        while k0 < spare:
+            in_order.append((k0, k0 ^ small))
+            k0 += 1
+        f_now = lax.ppermute(a_next, across, in_order)
+        state_next = latest & small == 0
+        a_next = jnp.concatenate(
+            [jnp.where(state_next, a_next, f_now), jnp.where(state_next, f_now, a_next)]
+        )
+        small *= 2
+    return a_next
+
+
+def fit_screen_over_axis(chunk, u, dim_at):
+    mid_arr = solve_the_notes(replace_panels(chunk, u), dim_at)
+    return mid_arr
+
+
+draft_the_groups = functools.partial(fit_screen_over_axis, u="ctx", dim_at=1)
 
 
 def exact_gelu(hidden):
@@ -171,9 +205,7 @@
     keys_values = jnp.concatenate(
         (qkv[:, width : 2 * width], qkv[:, 2 * width :] + bias_value), axis=1
     ).astype(BF16)
-    keys_values_all = lax.all_gather(
-        keys_values.reshape(group, block_len, 2 * width), "ctx", axis=1, tiled=True
-    )
+    keys_values_all = draft_the_groups(keys_values.reshape(group, block_len, 2 * width))
     keys_all = keys_values_all[:, :, :width]
     values_all = keys_values_all[:, :, width:]
     queries3 = queries.reshape(group, block_len, width)

time: 1160 us -> 1120 us (0.966)
  waiting for transfers between devices: 876 us -> 835 us
    all_gather x4, waiting for transfers between devices: 320 us -> 261 us  [gather_rows(): return lax.all_gather(part, 'fsdp', axis=0, tiled=True)]
    ppermute x0 -> x2, waiting for transfers between devices: none -> 44.9 us  [replace_panels(): f_now = lax.ppermute(a_next, across, in_order)]
    all_gather x1 -> x0, waiting for transfers between devices: 28.1 us -> none  [body(): lax.all_gather(keys_values.reshape(group, block_len, 2 * width), 'ctx', a...]
    unnamed x70 -> x90, local copies, waits for them, and re-layouts: 31.4 us -> 25.9 us
    unnamed x12 -> x11, waiting for transfers between devices: 99.2 us -> 100 us
  transfers between devices with their start and end apart: 11 -> 12, of which waited for: 11 -> 11; matrix products, arithmetic and copies ran while one was open for 8% -> 8% of each run, Pallas kernels for 0% -> 0%
where the time goes in v1:
time: 1120 us; the launch traced here: 1110 us
  waiting for transfers between devices  835 us (75%)
  matrix products  98.8 us (9%)
  blocking collectives  74.5 us (7%)
  local copies, waits for them, and re-layouts  55.4 us (5%)
  other arithmetic  30.1 us (3%)
  between operations  15.3 us (1%)
    reduce_scatter x3, waiting for transfers between devices, reduce_rows(): lax.psum_scatter(part.astype(BF16), 'fsdp', scatter_dimension=0, tiled=True)  373 us
    all_gather x4, waiting for transfers between devices, gather_rows(): return lax.all_gather(part, 'fsdp', axis=0, tiled=True)  261 us
    unnamed x11, waiting for transfers between devices  100 us
    ppermute x2, waiting for transfers between devices, replace_panels(): f_now = lax.ppermute(a_next, across, in_order)  44.9 us
    unnamed x1, blocking collectives  35.6 us
    reduce_scatter x1, waiting for transfers between devices, body(): lax.psum_scatter(jnp.concatenate((key_part, value_part), axis=2), 'ctx',...  34 us
    all_gather x1, blocking collectives, body(): lax.all_gather(jnp.concatenate(vectors), 'fsdp', axis=0, tiled=False)  32.9 us
    dot_general x4, matrix products, plain_product(): return jnp.dot(left, right, preferred_element_type=F32)  30 us
  transfers between devices with their start and end apart: 12, of which 11 were waited for; matrix products, arithmetic and copies ran while one was open for 8% of the time, Pallas kernels for 0%

profile of v1, /device:TPU:0, one launch (start us, length us, event | category | flops | bytes accessed | tf_op | source)
XLA Modules:
  0.0 1111.5 jit_solution(11913683890049771337)
XLA Ops:
  7.3 2.1 pad_maximum_fusion.7
  13.6 32.9 %all-gather.1 = bf16[8,1,1536]{2,1,0:T(2,128)(2,1)S(1)} all-gather(bf16[1,1,1536]{2,1,0:T(2,128)(2,1)S(1)} %reshape.351), channel_id=2, replica_groups=mesh['ctx'=4,'fsdp'=8] {'fsdp'}, dimensions={0}, use_global_device_ids=true | all-gather | bytes 27648 | tf_op jit(solution)/shard_map/all_gather | solution.py:176
  46.5 66.6 %all-gather.7.cloned.1.call-done = bf16[1024,3072]{1,0:T(8,128)(2,1)} async-done(((bf16[128,3072]{1,0:T(8,128)(2,1)}), bf16[1024,3072]{1,0:T(8,128)(2,1)}) %all-gather.7.cloned.1.call-update) | async-done | bytes 6291472 | tf_op jit(solution)/shard_map/all_gather | solution.py:136
  113.1 4.6 convolution_bitcast_fusion
  119.8 2.7 collective-permute-done
  127.9 2.3 reshape.358
  131.7 42.1 %collective-permute-done.1 = bf16[2,2,128,2048]{3,2,0,1:T(8,128)(2,1)} collective-permute-done((bf16[2,2,128,2048]{3,2,0,1:T(8,128)(2,1)}, bf16[2,2,128,2048]{3,2,0,1:T(8,128)(2,1)}, u32[]{:S(2)}, u32[]{:S(2)}) %collective-permute-start.1) | collective-permute-done | bytes 2097184 | tf_op jit(solution)/shard_map/ppermute | solution.py:29
  173.9 1.9 broadcast_select_fusion.1
  176.1 1.9 fusion.52
  178.0 2.5 copy.68
  180.5 2.9 copy.66
  183.4 7.6 fusion.54
  191.1 3.9 divide_convert_fusion
  195.0 2.0 copy-done
  199.8 2.7 fusion.55
  202.8 85.5 %all-gather.11.cloned.1.call-done = bf16[1024,4096]{1,0:T(8,128)(2,1)} async-done(((bf16[128,4096]{1,0:T(8,128)(2,1)}), bf16[1024,4096]{1,0:T(8,128)(2,1)}) %all-gather.11.cloned.1.call-update) | async-done | bytes 8388624 | tf_op jit(solution)/shard_map/all_gather | solution.py:136
  288.3 16.2 %multiply_convert_fusion.1 = (bf16[256,4096]{1,0:T(8,128)(2,1)}, f32[256,4096]{1,0:T(8,128)}, f32[256,4096]{1,0:T(8,128)}) fusion(f32[4096]{0:T(1024)S(1)} %bitcast.191, bf16[1024,4096]{1,0:T(8,128)(2,1)} %all-gather.11.cloned.1.call-done, f32[256,1024]{1,0:T(8,128)S(1)} %get-tuple-element.119, f32[1024]{0:T(1024)S(1)} %get-tuple-element.101, ...), kind=kOutput, calls=%fused_computation.20 | convolution fusion | flops 2218000384 | bytes 19949568 | tf_op jit(solution)/shard_map/dot_general | solution.py:51
  304.5 108.9 %all-gather.13.cloned.1.call-done = bf16[4096,1024]{1,0:T(8,128)(2,1)} async-done(((bf16[512,1024]{1,0:T(8,128)(2,1)}), bf16[4096,1024]{1,0:T(8,128)(2,1)}) %all-gather.13.cloned.1.call-update) | async-done | bytes 8388624 | tf_op jit(solution)/shard_map/all_gather | solution.py:136
  413.3 6.5 fusion.56
  422.1 11.3 %convert_reduce_fusion = (f32[4096]{0:T(1024)S(1)}, bf16[256,4096]{1,0:T(8,128)(2,1)S(1)}) fusion(f32[256,4096]{1,0:T(8,128)S(1)} %copy-done.31, f32[256,4096]{1,0:T(8,128)} %get-tuple-element.120, bf16[4096,1024]{1,0:T(8,128)(2,1)} %all-gather.13.cloned.1.call-done, f32[256,1024]{1,0:T(8,128)S(1)} %get-tuple-element.81), kind=kOutput, calls=%fused_computation.17 | convolution fusion | flops 2164518912 | bytes 19939328 | tf_op jit(solution)/shard_map/dot_general | solution.py:59
  433.5 6.9 multiply_reduce_fusion.1
  443.3 2.5 reshape.359
  445.7 2.8 copy.72
  448.5 4.0 fusion.1
  453.2 4.3 fusion.2
  457.5 1.9 copy-done.2
  459.4 2.0 multiply_convert_fusion
  461.5 4.0 copy.76
  465.4 2.4 copy.77
  467.9 4.7 pad_maximum_fusion.1
  474.2 4.6 convert_reduce_fusion.4
  478.8 1.9 copy.84
  481.4 34.0 %reduce-scatter.8.cloned.1.call-done = bf16[2,128,2048]{2,1,0:T(8,128)(2,1)} async-done(((bf16[2,512,2048]{2,1,0:T(8,128)(2,1)}), bf16[2,128,2048]{2,1,0:T(8,128)(2,1)}) %reduce-scatter.8.cloned.1.call-update) | async-done | bytes 1048592 | tf_op jit(solution)/shard_map/reduce_scatter | solution.py:246
  515.5 5.8 convert_bitcast_fusion
  521.3 8.6 copy.85
  531.3 2.0 convolution_convert_fusion.3
  533.4 7.5 convolution_convert_fusion
  540.9 7.3 convolution_convert_fusion.1
  549.7 98.3 %reduce-scatter.16.cloned.1.call-done = bf16[128,3072]{1,0:T(8,128)(2,1)} async-done(((bf16[1024,3072]{1,0:T(8,128)(2,1)}), bf16[128,3072]{1,0:T(8,128)(2,1)}) %reduce-scatter.16.cloned.1.call-update) | async-done | bytes 786448
  648.0 2.3 copy.86
  650.3 69.3 %reduce-scatter.10.cloned.1.call-done = bf16[128,1024]{1,0:T(8,128)(2,1)} async-done(((bf16[1024,1024]{1,0:T(8,128)(2,1)}), bf16[128,1024]{1,0:T(8,128)(2,1)}) %reduce-scatter.10.cloned.1.call-update) | async-done | bytes 262160 | tf_op jit(solution)/shard_map/reduce_scatter | solution.py:140
  719.6 152.1 %reduce-scatter.14.cloned.1.call-done = bf16[512,1024]{1,0:T(8,128)(2,1)} async-done(((bf16[4096,1024]{1,0:T(8,128)(2,1)}), bf16[512,1024]{1,0:T(8,128)(2,1)}) %reduce-scatter.14.cloned.1.call-update) | async-done | bytes 1048592 | tf_op jit(solution)/shard_map/reduce_scatter | solution.py:140
  871.8 151.7 %reduce-scatter.12.cloned.1.call-done = bf16[128,4096]{1,0:T(8,128)(2,1)} async-done(((bf16[1024,4096]{1,0:T(8,128)(2,1)}), bf16[128,4096]{1,0:T(8,128)(2,1)}) %reduce-scatter.12.cloned.1.call-update) | async-done | bytes 1048592 | tf_op jit(solution)/shard_map/reduce_scatter | solution.py:140
  1023.5 35.6 %all-reduce = f32[8,1536]{1,0:T(8,128)S(1)} all-reduce(f32[8,1536]{1,0:T(8,128)S(1)} %constant_dynamic-update-slice_fusion), channel_id=6, replica_groups=mesh['ctx'=4,'fsdp'=8] {'fsdp'}, use_global_device_ids=true, to_apply=%region_25.26.clone | all-reduce | flops 12288 | bytes 98304
  1059.8 6.0 psum.37
  1067.0 5.9 convolution_add_fusion.2
  1072.9 21.8 %all-reduce.4.cloned.1.call-done = (bf16[128,3072]{0,1:T(8,128)(2,1)}, bf16[128,1024]{1,0:T(8,128)(2,1)}, bf16[128,4096]{1,0:T(8,128)(2,1)}, bf16[512,1024]{1,0:T(8,128)(2,1)}) async-done(((bf16[128,3072]{0,1:T(8,128)(2,1)}, bf16[128,1024]{1,0:T(8,128)(2,1)}, bf16[128,4096]{1,0:T(8,128)(2,1)}, bf16[512,1024]{1,0:T(8,128)(2,1)}), (bf16[128,3072]{0,1:T(8,128)(2,1)}, bf16[128,1024]{1,0:T(8,128)(2,1)}, ...) | async-done | bytes 3145744 | tf_op jit(solution)/shard_map/psum | solution.py:141
  1099.0 2.8 convert_element_type.284
  (150 shorter events, 36.0 us)
Async XLA Ops:
  7.2 4.4 copy-start.22
  7.2 4.7 copy-start.23
  7.2 4.9 copy-start.24
  7.2 5.1 copy-start.25
  7.2 5.3 copy-start.26
  7.2 5.5 copy-start.21
  7.3 5.7 copy-start.27
  7.3 5.9 copy-start.28
  7.3 6.1 copy-start.29
  7.3 105.8 %copy-start.17 = (bf16[2,1,128,1024]{3,2,1,0:T(8,128)(2,1)S(1)}, bf16[2,1,128,1024]{3,2,1,0:T(8,128)(2,1)}, u32[]{:S(2)}) copy-start(bf16[2,1,128,1024]{3,2,1,0:T(8,128)(2,1)} %param.18) | copy-start | bytes 1572868
  7.3 105.8 %all-gather.7.cloned.1.call-start = ((), (), s32[]{:S(2)}) async-start(), calls=%async_computation.5 | async-start | bytes 7077888 | tf_op jit(solution)/shard_map/all_gather | solution.py:136
  9.5 190.3 %all-gather.9.cloned.1.call-start = ((), (), s32[]{:S(2)}) async-start(), calls=%async_computation.6 | async-start | bytes 2359296 | tf_op jit(solution)/shard_map/all_gather | solution.py:136
  10.2 278.1 %all-gather.11.cloned.1.call-start = ((), (), s32[]{:S(2)}) async-start(), calls=%async_computation.7 | async-start | bytes 9437184 | tf_op jit(solution)/shard_map/all_gather | solution.py:136
  11.0 402.4 %all-gather.13.cloned.1.call-start = ((), (), s32[]{:S(2)}) async-start(), calls=%async_computation.8 | async-start | bytes 9437184 | tf_op jit(solution)/shard_map/all_gather | solution.py:136
  11.6 503.9 %reduce-scatter.8.cloned.1.call-start = ((), (), s32[]{:S(2)}) async-start(), calls=%async_computation.9 | async-start | bytes 5242880 | tf_op jit(solution)/shard_map/reduce_scatter | solution.py:246
  118.8 0.8 copy-start.10
  119.7 2.9 collective-permute-start
  119.8 7.6 copy-start.20
  119.8 7.7 copy-start.8
  125.9 48.0 %collective-permute-start.1 = (bf16[2,2,128,2048]{3,2,0,1:T(8,128)(2,1)}, bf16[2,2,128,2048]{3,2,0,1:T(8,128)(2,1)}, u32[]{:S(2)}, u32[]{:S(2)}) collective-permute-start(bf16[2,2,128,2048]{3,2,0,1:T(8,128)(2,1)} %pad_maximum_fusion.2), channel_id=1, source_target_pairs={{0,16},{8,24},{16,0},{24,8},{1,17},{9,25},{17,1},{25,9},{2,18},{10... | collective-permute-start | bytes 6291464 | tf_op jit(solution)/shard_map/ppermute | solution.py:29
  180.5 2.9 copy-start.14
  195.0 2.0 copy-start
  413.3 6.8 copy-start.9
  419.9 2.2 copy-start.31
  422.0 11.4 %copy-start.12 = (f32[256,1024]{1,0:T(8,128)}, f32[256,1024]{1,0:T(8,128)S(1)}, u32[]{:S(2)}) copy-start(f32[256,1024]{1,0:T(8,128)S(1)} %get-tuple-element.81) | copy-start | bytes 3145732
  433.4 6.9 copy-start.13
  433.4 8.3 copy-start.5
  440.7 1.0 copy-start.3
  448.5 4.0 copy-start.1
  448.5 4.0 copy-start.11
  453.2 6.2 copy-start.15
  457.5 1.9 copy-start.2
  472.6 1.6 copy-start.6
  472.6 175.5 %reduce-scatter.16.cloned.1.call-start = ((), (), s32[]{:S(2)}) async-start(), calls=%async_computation.13 | async-start | bytes 7077888
  529.9 1.2 copy-start.4
  529.9 1.4 copy-start.7
  529.9 189.7 %reduce-scatter.10.cloned.1.call-start = ((), (), s32[]{:S(2)}) async-start(), calls=%async_computation.10 | async-start | bytes 2359296 | tf_op jit(solution)/shard_map/reduce_scatter | solution.py:140
  533.3 338.4 %reduce-scatter.14.cloned.1.call-start = ((), (), s32[]{:S(2)}) async-start(), calls=%async_computation.12 | async-start | bytes 9437184 | tf_op jit(solution)/shard_map/reduce_scatter | solution.py:140
  540.9 482.6 %reduce-scatter.12.cloned.1.call-start = ((), (), s32[]{:S(2)}) async-start(), calls=%async_computation.11 | async-start | bytes 9437184 | tf_op jit(solution)/shard_map/reduce_scatter | solution.py:140
  548.2 0.7 copy-start.30
  548.3 1.3 copy-start.19
  548.3 546.4 %all-reduce.4.cloned.1.call-start = ((), (), s32[]{:S(2)}) async-start(), calls=%async_computation.14 | async-start | bytes 6291456 | tf_op jit(solution)/shard_map/psum | solution.py:141
  1094.7 7.1 copy-start.16
  1097.0 6.3 copy-start.18
Sparse Core Ops, SparseCore 0:
  10.9 102.1 all-gather.6
  115.2 47.4 all-gather.8
  164.8 123.4 all-gather.10
  290.3 123.0 all-gather.12
  472.7 42.7 reduce-scatter.7
  530.1 117.9 reduce-scatter.15
  652.6 67.0 reduce-scatter.9
  723.7 148.0 reduce-scatter.13
  875.4 148.0 reduce-scatter.11
  1026.7 67.9 all-reduce.3
